TPU v7x, 512 devices: a whole 4x8x8 slice. The times are simulated.
512 devices in a mesh: dp: 32 (over x, y), expert: 2 (over core), ffn: 8 (over z).
Axes of the slice: x: 4, y: 8, z: 8, core: 2. Of those that a mesh axis runs over, the one named last changes fastest.
Arguments:
- grad_rows: bfloat16 [4096, 6144], P('dp', 'ffn'), may hold values from -80 to 80
- gate_probs: float32 [4096, 2], P('dp'), may hold values from 0.1 to 1
- expert_ids: int32 [4096, 2], P('dp'), may hold values from 0 to 3, all different within a row; in each aligned block of 128 rows (0 to 127, 128 to 255, ...) at most 72 rows name the same one
- gate_pre: bfloat16 [4, 2304, 8192], P('expert', 'ffn', 'dp'), may hold values from -6 to 6
- up_pre: bfloat16 [4, 2304, 8192], P('expert', 'ffn', 'dp'), may hold values from -40 to 40
- down_weight: bfloat16 [4, 8192, 6144], P('expert', 'dp', 'ffn'), may hold values from -0.0625 to 0.0625
Outputs:
- down_grad: bfloat16 [4, 8192, 6144], P('expert', 'dp', 'ffn')
- gate_grad: bfloat16 [4, 2304, 8192], P('expert', 'ffn', 'dp')
- up_grad: bfloat16 [4, 2304, 8192], P('expert', 'ffn', 'dp')
Inputs may be any that keep to these rules, and one draw needn't show every extreme that they name: `expert_ids`: in the 128 tokens of one index of dp no expert is named by more than 72 routes, a bound that some block reaches; a token's two routes name different experts.
All inputs are finite; a program needn't handle non-finite values.
Results may differ from a plain program's by a relative error of at most 0.019.
Values may be sent and summed in bfloat16 or wider, within the bound.
No kernel may reach another device: no remote copies, remote signals or barrier semaphores. Data moves between devices by JAX's collectives and lax.ppermute only.
A program may use at most 64 MiB of HBM per device.

v0:
```python
import math
import jax
import jax.numpy as jnp
from jax import lax
from jax.sharding import PartitionSpec as P

CAP = 72


def slot_table(route_ids, experts_total):
    tokens_here, routes = route_ids.shape
    flat_ids = route_ids.reshape(tokens_here * routes)
    one_hot = (flat_ids[:, None] == jnp.arange(experts_total, dtype=jnp.int32)[None, :]).astype(
        jnp.int32
    )
    earlier = jnp.cumsum(one_hot, axis=0) - one_hot
    return jnp.sum(earlier * one_hot, axis=1).reshape(tokens_here, routes)


def on_device(grad_rows, gate_probs, expert_ids, gate_pre, up_pre, down_weight):
    experts_here, rows_here, hidden_width = gate_pre.shape
    feature_width = down_weight.shape[2]
    capacity = CAP
    experts_total = experts_here * lax.axis_size("expert")
    slot_index = slot_table(expert_ids, experts_total)
    first_expert = lax.axis_index("expert") * experts_here
    local_ids = expert_ids - first_expert
    expert_match = (
        local_ids[:, :, None] == jnp.arange(experts_here, dtype=jnp.int32)[None, None, :]
    ).astype(jnp.float32)
    expert_match = expert_match * gate_probs[:, :, None]
    slot_match = (
        slot_index[:, :, None] == jnp.arange(capacity, dtype=jnp.int32)[None, None, :]
    ).astype(jnp.float32)
    placing = jnp.einsum("tke,tks->est", expert_match, slot_match, precision=lax.Precision.HIGHEST)
    dispatched = jnp.einsum(
        "est,td->esd", placing, grad_rows.astype(jnp.float32), precision=lax.Precision.HIGHEST
    ).astype(jnp.bfloat16)
    arrived = lax.all_gather(dispatched, "dp", axis=1, tiled=True)
    gate_value = gate_pre.astype(jnp.float32)
    up_value = up_pre.astype(jnp.float32)
    sigmoid_gate = jax.nn.sigmoid(gate_value)
    silu_gate = gate_value * sigmoid_gate
    hidden = (silu_gate * up_value).astype(jnp.bfloat16)
    partial_sums = jnp.einsum(
        "erd,efd->erf", arrived, down_weight, preferred_element_type=jnp.float32
    )
    own_rows = lax.psum_scatter(
        partial_sums.astype(jnp.bfloat16), "ffn", scatter_dimension=1, tiled=True
    ).astype(jnp.float32)
    gate_grad = (
        own_rows * up_value * sigmoid_gate * (1.0 + gate_value * (1.0 - sigmoid_gate))
    ).astype(jnp.bfloat16)
    up_grad = (own_rows * silu_gate).astype(jnp.bfloat16)
    weight_grad = jnp.einsum(
        "erf,erd->efd",
        lax.all_gather(hidden, "ffn", axis=1, tiled=True),
        arrived,
        preferred_element_type=jnp.float32,
    )
    squares = lax.psum(jnp.sum(weight_grad * weight_grad), ("dp", "expert", "ffn"))
    entry_count = (
        float(experts_total)
        * float(hidden_width * lax.axis_size("dp"))
        * float(feature_width * lax.axis_size("ffn"))
    )
    clip_limit = jnp.float32(0.5 * math.sqrt(entry_count))
    factor = clip_limit / jnp.maximum(jnp.sqrt(squares), clip_limit)
    down_grad = (weight_grad * factor).astype(jnp.bfloat16)
    return (down_grad, gate_grad, up_grad)


def solution(mesh):
    placed = (
        P("dp", "ffn"),
        P("dp", None),
        P("dp", None),
        P("expert", "ffn", "dp"),
        P("expert", "ffn", "dp"),
        P("expert", "dp", "ffn"),
    )
    return jax.shard_map(
        on_device,
        mesh=mesh,
        in_specs=placed,
        out_specs=(P("expert", "dp", "ffn"), P("expert", "ffn", "dp"), P("expert", "ffn", "dp")),
        check_vma=False,
    )
```

profile of v0, /device:TPU:1, one launch (start us, length us, event | category | flops | bytes accessed | tf_op | source)
XLA Modules:
  0.0 325.6 jit_solution(6122541284965118763)
XLA Ops:
  7.2 0.9 copy.13
  8.1 0.1 eq.57
  8.3 0.1 eq.53
  8.4 0.7 broadcast_subtract_fusion
  9.1 0.1 copy.17
  9.2 1.2 reduce-window.6
  10.4 0.1 slice.8
  10.5 0.1 copy.15
  10.7 0.1 copy.16
  10.8 0.1 add_bitcast_fusion
  10.9 0.1 eq.61
  11.0 0.8 copy.18
  11.8 1.1 fusion.9
  12.9 0.1 copy.19
  13.0 1.0 convolution_convert_fusion.1
  14.1 0.0 reduce-scatter.2.cloned.1.call-start
  14.1 102.3 %all-gather.5.cloned.1.call-done = bf16[2,2304,768]{2,1,0:T(8,128)(2,1)} async-done(((bf16[2,72,768]{2,1,0:T(8,128)(2,1)}), bf16[2,2304,768]{2,1,0:T(8,128)(2,1)}) %all-gather.5.cloned.1.call-update) | async-done | bytes 7077904 | tf_op jit(solution)/shard_map/all_gather | solution.py:39
  116.4 6.5 %convolution_convert_fusion = bf16[2,2304,256]{2,1,0:T(8,128)(2,1)} fusion(bf16[2,2304,768]{2,1,0:T(8,128)(2,1)} %all-gather.5.cloned.1.call-done, bf16[2,256,768]{2,1,0:T(8,128)(2,1)S(1)} %copy-done), kind=kOutput, calls=%fused_computation | convolution fusion | flops 1813118976 | bytes 10223616 | tf_op jit(solution)/shard_map/erd,efd->erf/dot_general | solution.py:45
  123.0 40.2 %reduce-scatter.2.cloned.1.call-done = bf16[2,288,256]{2,1,0:T(8,128)(2,1)} async-done(((bf16[2,2304,256]{2,1,0:T(8,128)(2,1)}), bf16[2,288,256]{2,1,0:T(8,128)(2,1)}) %reduce-scatter.2.cloned.1.call-update) | async-done | bytes 294928 | tf_op jit(solution)/shard_map/reduce_scatter | solution.py:48
  163.3 2.3 fusion.4
  165.6 45.2 %all-gather.3.cloned.1.call-done = bf16[2,2304,256]{2,1,0:T(8,128)(2,1)} async-done(((bf16[2,288,256]{2,1,0:T(8,128)(2,1)}), bf16[2,2304,256]{2,1,0:T(8,128)(2,1)}) %all-gather.3.cloned.1.call-update) | async-done | bytes 2359312 | tf_op jit(solution)/shard_map/all_gather | solution.py:57
  210.9 6.5 %multiply_reduce_fusion = (f32[]{:T(128)}, f32[2,256,768]{2,1,0:T(8,128)S(1)}) fusion(bf16[2,2304,256]{2,1,0:T(8,128)(2,1)} %all-gather.3.cloned.1.call-done, bf16[2,2304,768]{2,1,0:T(8,128)(2,1)} %all-gather.5.cloned.1.call-done), kind=kOutput, calls=%fused_computation.2 | convolution fusion | flops 1812725760 | bytes 11010052 | tf_op jit(solution)/shard_map/erf,erd->efd/dot_general | solution.py:55
  217.4 100.0 %psum.7 = f32[]{:T(128)} all-reduce(f32[]{:T(128)} %get-tuple-element.6), channel_id=1, replica_groups=mesh['dp'=32,'expert'=2,'ffn'=8] {'dp','expert','ffn'}, use_global_device_ids=true, to_apply=%region_4.5 | all-reduce | flops 1 | bytes 8 | tf_op jit(solution)/shard_map/psum | solution.py:61
  318.1 1.0 multiply_convert_fusion
  (17 shorter events, 0.2 us)
Async XLA Ops:
  7.2 109.3 %copy-start = (bf16[2,256,768]{2,1,0:T(8,128)(2,1)S(1)}, bf16[2,256,768]{2,1,0:T(8,128)(2,1)}, u32[]{:S(2)}) copy-start(bf16[2,256,768]{2,1,0:T(8,128)(2,1)} %param.11) | copy-start | bytes 2359300
  7.2 5.9 %copy-start.3 = (bf16[128,768]{1,0:T(8,128)(2,1)S(1)}, bf16[128,768]{1,0:T(8,128)(2,1)}, u32[]{:S(2)}) copy-start(bf16[128,768]{1,0:T(8,128)(2,1)} %param.6) | copy-start | bytes 589828
  7.2 109.3 %all-gather.5.cloned.1.call-start = ((), (), s32[]{:S(2)}) async-start(), calls=%async_computation.2 | async-start | bytes 7299072 | tf_op jit(solution)/shard_map/all_gather | solution.py:39
  14.1 149.2 %reduce-scatter.2.cloned.1.call-start = ((), (), s32[]{:S(2)}) async-start(), calls=%async_computation.3 | async-start | bytes 2654208 | tf_op jit(solution)/shard_map/reduce_scatter | solution.py:48
  123.0 40.3 %copy-start.1 = (bf16[2,288,256]{2,1,0:T(8,128)(2,1)S(1)}, bf16[2,288,256]{2,1,0:T(8,128)(2,1)}, u32[]{:S(2)}) copy-start(bf16[2,288,256]{2,1,0:T(8,128)(2,1)} %param.9) | copy-start | bytes 884740
  123.0 40.3 %copy-start.2 = (bf16[2,288,256]{2,1,0:T(8,128)(2,1)S(1)}, bf16[2,288,256]{2,1,0:T(8,128)(2,1)}, u32[]{:S(2)}) copy-start(bf16[2,288,256]{2,1,0:T(8,128)(2,1)} %param.10) | copy-start | bytes 884740
  123.0 87.9 %all-gather.3.cloned.1.call-start = ((), (), s32[]{:S(2)}) async-start(), calls=%async_computation.1 | async-start | bytes 2654208 | tf_op jit(solution)/shard_map/all_gather | solution.py:57
Sparse Core Ops, SparseCore 0:
  14.2 102.1 all-gather.4
  123.1 40.1 reduce-scatter.1
  165.9 44.8 all-gather.2
where the time goes:
time: 326 us
  waiting for transfers between devices  188 us (58%)
  blocking collectives  100 us (31%)
  matrix products  15.2 us (5%)
  between operations  14.5 us (4%)
  other arithmetic  5.35 us (2%)
    all_gather x1, waiting for transfers between devices, on_device(): arrived = lax.all_gather(dispatched, 'dp', axis=1, tiled=True)  102 us
    psum x1, blocking collectives, on_device(): lax.psum(jnp.sum(weight_grad * weight_grad), ('dp', 'expert', 'ffn'))  100 us
    all_gather x1, waiting for transfers between devices, on_device(): lax.all_gather(hidden, 'ffn', axis=1, tiled=True)  45.2 us
    reduce_scatter x1, waiting for transfers between devices, on_device(): lax.psum_scatter(partial_sums.astype(jnp.bfloat16), 'ffn', scatter_dimens...  40.2 us
    dot_general x1, matrix products, on_device(): jnp.einsum('erf,erd->efd', lax.all_gather(hidden, 'ffn', axis=1, tiled=Tr...  6.55 us
  transfers between devices with their start and end apart: 3, of which 3 were waited for; matrix products, arithmetic and copies ran while one was open for 0% of the time, Pallas kernels for 0%

commit v1 on v0

--- a/solution.py
+++ b/solution.py
@@ -5,6 +5,22 @@
 from jax.sharding import PartitionSpec as P
 
 CAP = 72
+
+
+def summed_both_ways(x, axis, dim, product):
+    size, place, width = (lax.axis_size(axis), lax.axis_index(axis), x.shape[dim])
+    right = [(i, (i + 1) % size) for i in range(size)]
+    left = [(i, (i - 1) % size) for i in range(size)]
+    middle = size // 2
+    from_left = from_right = x
+    total = product(x, place * width)
+    for turn in range(1, middle + 1):
+        from_left = lax.ppermute(from_left, axis, right)
+        if turn < size - middle:
+            from_right = lax.ppermute(from_right, axis, left)
+            total = total + product(from_right, (place + turn) % size * width)
+        total = total + product(from_left, (place - turn) % size * width)
+    return total
 
 
 def slot_table(route_ids, experts_total):
@@ -52,11 +68,16 @@
         own_rows * up_value * sigmoid_gate * (1.0 + gate_value * (1.0 - sigmoid_gate))
     ).astype(jnp.bfloat16)
     up_grad = (own_rows * silu_gate).astype(jnp.bfloat16)
-    weight_grad = jnp.einsum(
-        "erf,erd->efd",
-        lax.all_gather(hidden, "ffn", axis=1, tiled=True),
-        arrived,
-        preferred_element_type=jnp.float32,
+    weight_grad = summed_both_ways(
+        hidden,
+        "ffn",
+        1,
+        lambda shard, offset: jnp.einsum(
+            "erf,erd->efd",
+            shard,
+            lax.dynamic_slice_in_dim(arrived, offset, shard.shape[1], axis=1),
+            preferred_element_type=jnp.float32,
+        ),
     )
     squares = lax.psum(jnp.sum(weight_grad * weight_grad), ("dp", "expert", "ffn"))
     entry_count = (

time: 326 us -> 319 us (0.979)
  waiting for transfers between devices: 188 us -> 151 us
  starting transfers between devices: 0.12 us -> 21.6 us
  blocking collectives: 100 us -> 105 us
    all_gather x1 -> x0, waiting for transfers between devices: 45.2 us -> none  [on_device(): lax.all_gather(hidden, 'ffn', axis=1, tiled=True)]
    ppermute x0 -> x7, starting transfers between devices: none -> 21.5 us  [the longest x3 13.4 us: summed_both_ways(): from_right = lax.ppermute(from_right, axis, left)]
    ppermute x0 -> x7, waiting for transfers between devices: none -> 7.75 us  [the longest x4 7.74 us: summed_both_ways(): from_left = lax.ppermute(from_left, axis, right)]
    psum x1, blocking collectives: 100 us -> 105 us  [on_device(): lax.psum(jnp.sum(weight_grad * weight_grad), ('dp', 'expert', 'ffn'))]
    dot_general x1 -> x8, matrix products: 6.55 us -> 9.71 us  [on_device(): jnp.einsum('erf,erd->efd', shard, lax.dynamic_slice_in_dim(arrived, offse...]
  transfers between devices with their start and end apart: 3 -> 9, of which waited for: 3 -> 5; matrix products, arithmetic and copies ran while one was open for 0% -> 3% of each run, Pallas kernels for 0% -> 0%
where the time goes in v1:
time: 319 us
  waiting for transfers between devices  151 us (47%)
  blocking collectives  105 us (33%)
  starting transfers between devices  21.6 us (7%)
  matrix products  18.4 us (6%)
  between operations  15.1 us (5%)
  other arithmetic  5.17 us (2%)
    psum x1, blocking collectives, on_device(): lax.psum(jnp.sum(weight_grad * weight_grad), ('dp', 'expert', 'ffn'))  105 us
    all_gather x1, waiting for transfers between devices, on_device(): arrived = lax.all_gather(dispatched, 'dp', axis=1, tiled=True)  102 us
    reduce_scatter x1, waiting for transfers between devices, on_device(): lax.psum_scatter(partial_sums.astype(jnp.bfloat16), 'ffn', scatter_dimens...  40.7 us
    ppermute x3, starting transfers between devices, summed_both_ways(): from_right = lax.ppermute(from_right, axis, left)  13.4 us
    dot_general x8, matrix products, on_device(): jnp.einsum('erf,erd->efd', shard, lax.dynamic_slice_in_dim(arrived, offse...  9.71 us
    ppermute x4, starting transfers between devices, summed_both_ways(): from_left = lax.ppermute(from_left, axis, right)  8.1 us
    ppermute x4, waiting for transfers between devices, summed_both_ways(): from_left = lax.ppermute(from_left, axis, right)  7.74 us
    dot_general x1, matrix products, on_device(): jnp.einsum('erd,efd->erf', arrived, down_weight, preferred_element_type=j...  6.51 us
  transfers between devices with their start and end apart: 9, of which 5 were waited for; matrix products, arithmetic and copies ran while one was open for 3% of the time, Pallas kernels for 0%

profile of v1, /device:TPU:1, one launch (start us, length us, event | category | flops | bytes accessed | tf_op | source)
XLA Modules:
  0.0 318.6 jit_solution(17496911375060153053)
XLA Ops:
  7.2 0.8 copy.13
  9.2 1.2 reduce-window.6
  11.0 0.8 copy.18
  11.8 1.1 fusion.24
  13.0 1.0 convolution_convert_fusion.1
  14.1 102.3 %all-gather.2.cloned.1.call-done = bf16[2,2304,768]{2,1,0:T(8,128)(2,1)} async-done(((bf16[2,72,768]{2,1,0:T(8,128)(2,1)}), bf16[2,2304,768]{2,1,0:T(8,128)(2,1)}) %all-gather.2.cloned.1.call-update) | async-done | bytes 7077904 | tf_op jit(solution)/shard_map/all_gather | solution.py:55
  116.4 6.5 %convolution_convert_fusion = bf16[2,2304,256]{2,1,0:T(8,128)(2,1)} fusion(bf16[2,2304,768]{2,1,0:T(8,128)(2,1)} %all-gather.2.cloned.1.call-done, bf16[2,256,768]{2,1,0:T(8,128)(2,1)S(1)} %copy-done), kind=kOutput, calls=%fused_computation | convolution fusion | flops 1813118976 | bytes 10223616 | tf_op jit(solution)/shard_map/erd,efd->erf/dot_general | solution.py:61
  122.9 40.7 %reduce-scatter.2.cloned.1.call-done = bf16[2,288,256]{2,1,0:T(8,128)(2,1)} async-done(((bf16[2,2304,256]{2,1,0:T(8,128)(2,1)}), bf16[2,288,256]{2,1,0:T(8,128)(2,1)}) %reduce-scatter.2.cloned.1.call-update) | async-done | bytes 294928 | tf_op jit(solution)/shard_map/reduce_scatter | solution.py:64
  163.6 2.1 fusion.19
  165.8 2.2 collective-permute-start.1
  168.0 4.3 %collective-permute-start = (bf16[2,288,256]{2,1,0:T(8,128)(2,1)S(1)}, bf16[2,288,256]{2,1,0:T(8,128)(2,1)S(1)}, u32[]{:S(2)}, u32[]{:S(2)}) collective-permute-start(bf16[2,288,256]{2,1,0:T(8,128)(2,1)S(1)} %get-tuple-element.5), channel_id=1, source_target_pairs={{0,7},{1,0},{2,1},{3,2},{4,3},{5,4},{6,5},{7,6},{8,15},{9,8},{10,9... | collective-permute-start | bytes 884744 | tf_op jit(solution)/shard_map/ppermute | solution.py:20
  172.4 1.9 fusion.13
  174.4 2.0 collective-permute-start.3
  176.5 4.6 %collective-permute-start.2 = (bf16[2,288,256]{2,1,0:T(8,128)(2,1)S(1)}, bf16[2,288,256]{2,1,0:T(8,128)(2,1)S(1)}, u32[]{:S(2)}, u32[]{:S(2)}) collective-permute-start(bf16[2,288,256]{2,1,0:T(8,128)(2,1)S(1)} %collective-permute-done), channel_id=1, source_target_pairs={{0,7},{1,0},{2,1},{3,2},{4,3},{5,4},{6,5},{7,6},{8,15},{9,8},{10,9... | collective-permute-start | bytes 884744 | tf_op jit(solution)/shard_map/ppermute | solution.py:20
  181.1 1.8 fusion.11
  182.9 1.8 fusion.9
  184.7 1.9 collective-permute-start.5
  186.6 4.6 %collective-permute-start.4 = (bf16[2,288,256]{2,1,0:T(8,128)(2,1)S(1)}, bf16[2,288,256]{2,1,0:T(8,128)(2,1)S(1)}, u32[]{:S(2)}, u32[]{:S(2)}) collective-permute-start(bf16[2,288,256]{2,1,0:T(8,128)(2,1)S(1)} %collective-permute-done.2), channel_id=1, source_target_pairs={{0,7},{1,0},{2,1},{3,2},{4,3},{5,4},{6,5},{7,6},{8,15},{9,8},{10,9... | collective-permute-start | bytes 884744 | tf_op jit(solution)/shard_map/ppermute | solution.py:20
  192.5 0.9 collective-permute-done.5
  193.4 1.9 collective-permute-start.6
  196.6 6.8 %collective-permute-done.6 = bf16[2,288,256]{2,1,0:T(8,128)(2,1)S(1)} collective-permute-done((bf16[2,288,256]{2,1,0:T(8,128)(2,1)S(1)}, bf16[2,288,256]{2,1,0:T(8,128)(2,1)S(1)}, u32[]{:S(2)}, u32[]{:S(2)}) %collective-permute-start.6) | collective-permute-done | bytes 294944 | tf_op jit(solution)/shard_map/ppermute | solution.py:18
  203.4 1.6 multiply_reduce_fusion
  205.0 105.1 %psum.7 = f32[]{:T(128)} all-reduce(f32[]{:T(128)} %get-tuple-element.6), channel_id=1, replica_groups=mesh['dp'=32,'expert'=2,'ffn'=8] {'dp','expert','ffn'}, use_global_device_ids=true, to_apply=%region_4.5 | all-reduce | flops 1 | bytes 8 | tf_op jit(solution)/shard_map/psum | solution.py:82
  310.8 1.0 multiply_convert_fusion
  (37 shorter events, 4.5 us)
Async XLA Ops:
  7.2 109.2 %copy-start = (bf16[2,256,768]{2,1,0:T(8,128)(2,1)S(1)}, bf16[2,256,768]{2,1,0:T(8,128)(2,1)}, u32[]{:S(2)}) copy-start(bf16[2,256,768]{2,1,0:T(8,128)(2,1)} %param.11) | copy-start | bytes 2359300
  7.2 109.2 %all-gather.2.cloned.1.call-start = ((), (), s32[]{:S(2)}) async-start(), calls=%async_computation.1 | async-start | bytes 7299072 | tf_op jit(solution)/shard_map/all_gather | solution.py:55
  11.7 1.2 copy-start.4
  14.0 149.6 %reduce-scatter.2.cloned.1.call-start = ((), (), s32[]{:S(2)}) async-start(), calls=%async_computation.2 | async-start | bytes 2654208 | tf_op jit(solution)/shard_map/reduce_scatter | solution.py:64
  122.9 40.7 %copy-start.2 = (bf16[2,288,256]{2,1,0:T(8,128)(2,1)S(1)}, bf16[2,288,256]{2,1,0:T(8,128)(2,1)}, u32[]{:S(2)}) copy-start(bf16[2,288,256]{2,1,0:T(8,128)(2,1)} %param.9) | copy-start | bytes 884740
  122.9 40.7 %copy-start.3 = (bf16[2,288,256]{2,1,0:T(8,128)(2,1)S(1)}, bf16[2,288,256]{2,1,0:T(8,128)(2,1)}, u32[]{:S(2)}) copy-start(bf16[2,288,256]{2,1,0:T(8,128)(2,1)} %param.10) | copy-start | bytes 884740
  165.8 8.7 %collective-permute-start.1 = (bf16[2,288,256]{2,1,0:T(8,128)(2,1)S(1)}, bf16[2,288,256]{2,1,0:T(8,128)(2,1)S(1)}, u32[]{:S(2)}, u32[]{:S(2)}) collective-permute-start(bf16[2,288,256]{2,1,0:T(8,128)(2,1)S(1)} %get-tuple-element.5), channel_id=1, source_target_pairs={{0,1},{1,2},{2,3},{3,4},{4,5},{5,6},{6,7},{7,0},{8,9},{9,10},{10,1... | collective-permute-start | bytes 884744 | tf_op jit(solution)/shard_map/ppermute | solution.py:18
  168.0 8.5 %collective-permute-start = (bf16[2,288,256]{2,1,0:T(8,128)(2,1)S(1)}, bf16[2,288,256]{2,1,0:T(8,128)(2,1)S(1)}, u32[]{:S(2)}, u32[]{:S(2)}) collective-permute-start(bf16[2,288,256]{2,1,0:T(8,128)(2,1)S(1)} %get-tuple-element.5), channel_id=1, source_target_pairs={{0,7},{1,0},{2,1},{3,2},{4,3},{5,4},{6,5},{7,6},{8,15},{9,8},{10,9... | collective-permute-start | bytes 884744 | tf_op jit(solution)/shard_map/ppermute | solution.py:20
  172.4 18.8 %copy-start.1 = (bf16[2,2304,768]{2,1,0:T(8,128)(2,1)S(1)}, bf16[2,2304,768]{2,1,0:T(8,128)(2,1)}, u32[]{:S(2)}) copy-start(bf16[2,2304,768]{2,1,0:T(8,128)(2,1)} %all-gather.2.cloned.1.call-done) | copy-start | bytes 21233668
  174.4 10.3 %collective-permute-start.3 = (bf16[2,288,256]{2,1,0:T(8,128)(2,1)S(1)}, bf16[2,288,256]{2,1,0:T(8,128)(2,1)S(1)}, u32[]{:S(2)}, u32[]{:S(2)}) collective-permute-start(bf16[2,288,256]{2,1,0:T(8,128)(2,1)S(1)} %collective-permute-done.1), channel_id=1, source_target_pairs={{0,1},{1,2},{2,3},{3,4},{4,5},{5,6},{6,7},{7,0},{8,9},{9,10},{10,1... | collective-permute-start | bytes 884744 | tf_op jit(solution)/shard_map/ppermute | solution.py:18
  176.5 10.1 %collective-permute-start.2 = (bf16[2,288,256]{2,1,0:T(8,128)(2,1)S(1)}, bf16[2,288,256]{2,1,0:T(8,128)(2,1)S(1)}, u32[]{:S(2)}, u32[]{:S(2)}) collective-permute-start(bf16[2,288,256]{2,1,0:T(8,128)(2,1)S(1)} %collective-permute-done), channel_id=1, source_target_pairs={{0,7},{1,0},{2,1},{3,2},{4,3},{5,4},{6,5},{7,6},{8,15},{9,8},{10,9... | collective-permute-start | bytes 884744 | tf_op jit(solution)/shard_map/ppermute | solution.py:20
  184.7 8.7 %collective-permute-start.5 = (bf16[2,288,256]{2,1,0:T(8,128)(2,1)S(1)}, bf16[2,288,256]{2,1,0:T(8,128)(2,1)S(1)}, u32[]{:S(2)}, u32[]{:S(2)}) collective-permute-start(bf16[2,288,256]{2,1,0:T(8,128)(2,1)S(1)} %collective-permute-done.3), channel_id=1, source_target_pairs={{0,1},{1,2},{2,3},{3,4},{4,5},{5,6},{6,7},{7,0},{8,9},{9,10},{10,1... | collective-permute-start | bytes 884744 | tf_op jit(solution)/shard_map/ppermute | solution.py:18
  186.6 9.3 %collective-permute-start.4 = (bf16[2,288,256]{2,1,0:T(8,128)(2,1)S(1)}, bf16[2,288,256]{2,1,0:T(8,128)(2,1)S(1)}, u32[]{:S(2)}, u32[]{:S(2)}) collective-permute-start(bf16[2,288,256]{2,1,0:T(8,128)(2,1)S(1)} %collective-permute-done.2), channel_id=1, source_target_pairs={{0,7},{1,0},{2,1},{3,2},{4,3},{5,4},{6,5},{7,6},{8,15},{9,8},{10,9... | collective-permute-start | bytes 884744 | tf_op jit(solution)/shard_map/ppermute | solution.py:20
  193.4 10.0 %collective-permute-start.6 = (bf16[2,288,256]{2,1,0:T(8,128)(2,1)S(1)}, bf16[2,288,256]{2,1,0:T(8,128)(2,1)S(1)}, u32[]{:S(2)}, u32[]{:S(2)}) collective-permute-start(bf16[2,288,256]{2,1,0:T(8,128)(2,1)S(1)} %collective-permute-done.5), channel_id=1, source_target_pairs={{0,1},{1,2},{2,3},{3,4},{4,5},{5,6},{6,7},{7,0},{8,9},{9,10},{10,1... | collective-permute-start | bytes 884744 | tf_op jit(solution)/shard_map/ppermute | solution.py:18
Sparse Core Ops, SparseCore 0:
  14.2 102.1 all-gather.1
  123.1 40.5 reduce-scatter.1
